TPU v7x, 32 devices: a whole 2x2x4 slice. The times are simulated.
32 devices in a mesh: wide: 8 (over z, y), narrow: 4 (over x, core).
Axes of the slice: x: 2, y: 2, z: 4, core: 2. Of those that a mesh axis runs over, the one named last changes fastest.
Arguments:
- desc_a: bfloat16 [4096, 128], P('wide'), may hold values from -6 to 6
- desc_b: bfloat16 [32768, 128], P('narrow'), may hold values from -6 to 6
- logmass_a: float32 [4096], P('wide'), may hold values from -6 to 6
- logmass_b: float32 [32768], P('narrow'), may hold values from -6 to 6
- g_start: float32 [32768], P('narrow'), may hold values from -1 to 16, as said below
Outputs:
- potential_a: float32 [4096], P('wide')
- potential_b: float32 [32768], P('narrow')
- flow_a: float32 [4096, 128], P('wide')
- flow_b: float32 [32768, 128], P(('narrow', 'wide'))
Inputs may be any that keep to these rules, and one draw needn't show every extreme that they name: `g_start`: potentials of view B carried over from the previous pair of views.
All inputs are finite; a program needn't handle non-finite values.
Results may differ from a plain program's by a relative error of at most 0.01.
Values may be sent and summed in bfloat16 or wider, within the bound.
A program may use at most 64 MiB of HBM per device.

v0:
```python
import jax
import jax.numpy as jnp
from jax import lax
from jax.sharding import PartitionSpec as P

ITERS = 2
EPS = 0.05


def combined_all(part, axis, combine):
    gathered = jax.tree.map(lambda a: lax.all_gather(a, axis), part)

    def take(source):
        return jax.tree.map(lambda a: lax.dynamic_index_in_dim(a, source, 0, False), gathered)

    return lax.fori_loop(
        1, lax.axis_size(axis), lambda source, state: combine(state, take(source)), take(0)
    )


def unit_rows(desc):
    wide32 = desc.astype(jnp.float32)
    return (wide32 / jnp.sqrt(jnp.sum(wide32 * wide32, axis=1, keepdims=True) + 1e-06)).astype(
        jnp.bfloat16
    )


def cost_of(left, right):
    return 2.0 - 2.0 * lax.dot_general(
        left, right, (((1,), (1,)), ((), ())), preferred_element_type=jnp.float32
    )


def left_product(weights, tile_a):
    return lax.dot_general(
        weights, tile_a, (((0,), (0,)), ((), ())), preferred_element_type=jnp.float32
    )


def pair_combine(first_pair, second_pair):
    new_high = jnp.maximum(first_pair[0], second_pair[0])
    summed = first_pair[1] * jnp.exp(first_pair[0] - new_high) + second_pair[1] * jnp.exp(
        second_pair[0] - new_high
    )
    return (new_high, summed)


def finish_rows(highest, summed):
    highest, summed = combined_all((highest, summed), "narrow", pair_combine)
    return highest + jnp.log(summed)


def finish_cols(highest, summed):
    highest, summed = combined_all((highest, summed), "wide", pair_combine)
    return highest + jnp.log(summed)


def row_update(state_now, pot_part, cost):
    highest, summed = state_now
    scores = (pot_part[None, :] - cost) / EPS
    new_high = jnp.maximum(highest, jnp.max(scores, axis=1))
    summed = summed * jnp.exp(highest - new_high) + jnp.sum(
        jnp.exp(scores - new_high[:, None]), axis=1
    )
    return (new_high, summed)


def on_device(desc_a, desc_b, logmass_a, logmass_b, g_start):
    unit_a = unit_rows(desc_a)
    unit_b = unit_rows(desc_b)
    n_rows, feat_width = unit_a.shape
    n_cols = unit_b.shape[0]
    col_span = min(n_cols, 2048)
    n_tiles = n_cols // col_span
    b_tiles = unit_b.reshape(n_tiles, col_span, feat_width)
    row_init = (jnp.full((n_rows,), -jnp.inf, jnp.float32), jnp.zeros((n_rows,), jnp.float32))

    def row_partial(potential):

        def row_one_tile(state_now, inputs):
            tile_b, pot_part = inputs
            return (row_update(state_now, pot_part, cost_of(unit_a, tile_b)), None)

        result, _ = lax.scan(
            row_one_tile, row_init, (b_tiles, potential.reshape(n_tiles, col_span))
        )
        return result

    potential_b = g_start
    for sweep_index in range(ITERS):
        row_pot = EPS * logmass_a - EPS * finish_rows(*row_partial(potential_b))

        def col_one_tile(tile_b):
            scores = (row_pot[:, None] - cost_of(unit_a, tile_b)) / EPS
            highest = jnp.max(scores, axis=0)
            return (highest, jnp.sum(jnp.exp(scores - highest[None, :]), axis=0))

        highest, summed = lax.map(col_one_tile, b_tiles)
        lse_b = finish_cols(*(highest.reshape(n_cols), summed.reshape(n_cols)))
        potential_b = EPS * logmass_b - EPS * lse_b
    my_share = n_cols // lax.axis_size("wide")
    first_row = lax.axis_index("wide") * my_share
    own_cols = lax.dynamic_slice_in_dim(unit_b, first_row, my_share, 0)

    def joint_tile(state_now, inputs):
        tile_b, pot_part, lse_part = inputs
        cost = cost_of(unit_a, tile_b)
        weights = jnp.exp((row_pot[:, None] - cost) / EPS - lse_part[None, :]).astype(jnp.bfloat16)
        return (row_update(state_now, pot_part, cost), left_product(weights, unit_a))

    row_stats, tile_sums = lax.scan(
        joint_tile,
        row_init,
        (b_tiles, potential_b.reshape(n_tiles, col_span), lse_b.reshape(n_tiles, col_span)),
    )
    lse_a = finish_rows(*row_stats)
    sums_b = lax.psum_scatter(
        tile_sums.reshape(n_cols, feat_width).astype(jnp.bfloat16),
        "wide",
        scatter_dimension=0,
        tiled=True,
    ).astype(jnp.float32)
    flow_b = sums_b - own_cols.astype(jnp.float32)
    potential_a = EPS * logmass_a - EPS * lse_a

    def flow_tile(acc_now, inputs):
        tile_b, pot_part = inputs
        weights = jnp.exp(
            (pot_part[None, :] - cost_of(unit_a, tile_b)) / EPS - lse_a[:, None]
        ).astype(jnp.bfloat16)
        return (acc_now + jnp.dot(weights, tile_b, preferred_element_type=jnp.float32), None)

    sums_a, _ = lax.scan(
        flow_tile,
        jnp.zeros((n_rows, feat_width), jnp.float32),
        (b_tiles, potential_b.reshape(n_tiles, col_span)),
    )
    sums_a = lax.psum(sums_a.astype(jnp.bfloat16), "narrow").astype(jnp.float32)
    flow_a = sums_a - unit_a.astype(jnp.float32)
    return (potential_a, potential_b, flow_a, flow_b)


def solution(mesh):
    return jax.shard_map(
        on_device,
        mesh=mesh,
        in_specs=(P("wide", None), P("narrow", None), P("wide"), P("narrow"), P("narrow")),
        out_specs=(P("wide"), P("narrow"), P("wide", None), P(("narrow", "wide"), None)),
        check_vma=False,
    )
```

profile of v0, /device:TPU:0, one launch (start us, length us, event | category | flops | bytes accessed | tf_op | source)
XLA Modules:
  0.0 360.6 jit_solution(10728813550272672152)
XLA Ops:
  8.1 2.7 fusion.36
  10.9 4.6 %fusion.37 = bf16[8192,128]{1,0:T(8,128)(2,1)S(1)} fusion(bf16[8192,128]{1,0:T(8,128)(2,1)} %param.28, f32[8192]{0:T(1024)S(1)} %add_sqrt_fusion), kind=kLoop, calls=%fused_computation.76 | loop fusion | flops 3145728 | bytes 4227072 | tf_op jit(solution)/shard_map/convert_element_type | solution.py:23
  15.8 22.7 %while.168 = (s32[]{:T(128)}, f32[512]{0:T(512)S(1)}, f32[512]{0:T(512)S(1)}, f32[4,2048]{1,0:T(4,128)S(1)}, bf16[4,2048,128]{2,1,0:T(8,128)(2,1)S(1)}, /*index=5*/bf16[512,128]{1,0:T(8,128)(2,1)S(1)}, s32[]{:T(128)}, s32[]{:T(128)}) while((s32[]{:T(128)}, f32[512]{0:T(512)S(1)}, f32[512]{0:T(512)S(1)}, f32[4,2048]{1,0:T(4,128)S(1)}, ...), condition=%wide.region_5.6_spmd.clone, body=%wide.region_2.5_spmd.clone.sunk | while | flops 275778048 | bytes 9095272 | solution.py:84
  15.9 2.8 fusion.75
  18.7 2.8 exponential_reduce_fusion.12
  21.5 2.8 fusion.75
  24.3 2.8 exponential_reduce_fusion.12
  27.2 2.8 fusion.75
  30.0 2.8 exponential_reduce_fusion.12
  32.9 2.8 fusion.75
  35.7 2.8 exponential_reduce_fusion.12
  38.5 6.2 %all-gather.6 = f32[4,1,512]{2,1,0:T(1,128)S(1)} all-gather(f32[1,1,512]{2,1,0:T(1,128)S(1)} %bitcast.198), channel_id=2, replica_groups=mesh['wide'=8,'narrow'=4] {'narrow'}, dimensions={0}, use_global_device_ids=true | all-gather | bytes 10240 | tf_op jit(solution)/shard_map/all_gather | solution.py:11
  44.7 5.5 %all-gather.7 = f32[4,1,512]{2,1,0:T(1,128)S(1)} all-gather(f32[1,1,512]{2,1,0:T(1,128)S(1)} %bitcast.217), channel_id=3, replica_groups=mesh['wide'=8,'narrow'=4] {'narrow'}, dimensions={0}, use_global_device_ids=true | all-gather | bytes 10240 | tf_op jit(solution)/shard_map/all_gather | solution.py:11
  50.4 7.3 %while.162 = (s32[]{:T(128)}, f32[4,2048]{1,0:T(4,128)S(1)}, f32[4,2048]{1,0:T(4,128)S(1)}, f32[512]{0:T(512)S(1)}, bf16[4,2048,128]{2,1,0:T(8,128)(2,1)S(1)}, /...) while((s32[]{:T(128)}, f32[4,2048]{1,0:T(4,128)S(1)}, f32[4,2048]{1,0:T(4,128)S(1)}, ...), condition=%wide.region_11.12_spmd, body=%wide.region_8.11_spmd.sunk | while | flops 275771392 | bytes 9103457 | solution.py:98
  57.8 31.4 %all-gather.8 = f32[8,1,8192]{2,1,0:T(1,128)S(1)} all-gather(f32[1,1,8192]{2,1,0:T(1,128)S(1)} %reshape.74), channel_id=1, replica_groups=mesh['wide'=8,'narrow'=4] {'wide'}, dimensions={0}, use_global_device_ids=true | all-gather | bytes 294912 | tf_op jit(solution)/shard_map/all_gather | solution.py:11
  89.4 30.7 %all-gather.9 = f32[8,1,8192]{2,1,0:T(1,128)S(1)} all-gather(f32[1,1,8192]{2,1,0:T(1,128)S(1)} %reshape.76), channel_id=1, replica_groups=mesh['wide'=8,'narrow'=4] {'wide'}, dimensions={0}, use_global_device_ids=true | all-gather | bytes 294912 | tf_op jit(solution)/shard_map/all_gather | solution.py:11
  121.2 22.7 %while.169 = (s32[]{:T(128)}, f32[512]{0:T(512)S(1)}, f32[512]{0:T(512)S(1)}, f32[4,2048]{1,0:T(4,128)S(1)}, bf16[4,2048,128]{2,1,0:T(8,128)(2,1)S(1)}, /*index=5*/bf16[512,128]{1,0:T(8,128)(2,1)S(1)}, s32[]{:T(128)}, s32[]{:T(128)}) while((s32[]{:T(128)}, f32[512]{0:T(512)S(1)}, f32[512]{0:T(512)S(1)}, ...), condition=%wide.region_17.18_spmd.clone, body=%wide.region_14.17_spmd.clone.sunk | while | flops 275778048 | bytes 9095272 | solution.py:84
  121.3 2.8 fusion.78
  124.1 2.8 exponential_reduce_fusion.13
  126.9 2.8 fusion.78
  129.7 2.8 exponential_reduce_fusion.13
  132.6 2.8 fusion.78
  135.4 2.8 exponential_reduce_fusion.13
  138.3 2.8 fusion.78
  141.1 2.8 exponential_reduce_fusion.13
  143.9 5.2 %all-gather.10 = f32[4,1,512]{2,1,0:T(1,128)S(1)} all-gather(f32[1,1,512]{2,1,0:T(1,128)S(1)} %bitcast.197), channel_id=4, replica_groups=mesh['wide'=8,'narrow'=4] {'narrow'}, dimensions={0}, use_global_device_ids=true | all-gather | bytes 10240 | tf_op jit(solution)/shard_map/all_gather | solution.py:11
  149.1 5.2 %all-gather.11 = f32[4,1,512]{2,1,0:T(1,128)S(1)} all-gather(f32[1,1,512]{2,1,0:T(1,128)S(1)} %bitcast.216), channel_id=5, replica_groups=mesh['wide'=8,'narrow'=4] {'narrow'}, dimensions={0}, use_global_device_ids=true | all-gather | bytes 10240 | tf_op jit(solution)/shard_map/all_gather | solution.py:11
  154.5 7.3 %while.165 = (s32[]{:T(128)}, f32[4,2048]{1,0:T(4,128)S(1)}, f32[4,2048]{1,0:T(4,128)S(1)}, f32[512]{0:T(512)S(1)}, bf16[4,2048,128]{2,1,0:T(8,128)(2,1)S(1)}, /...) while((s32[]{:T(128)}, f32[4,2048]{1,0:T(4,128)S(1)}, f32[4,2048]{1,0:T(4,128)S(1)}, ...), condition=%wide.region_23.24_spmd, body=%wide.region_20.23_spmd.sunk | while | flops 275771392 | bytes 9103457 | solution.py:98
  161.8 30.8 %all-gather.12 = f32[8,1,8192]{2,1,0:T(1,128)S(1)} all-gather(f32[1,1,8192]{2,1,0:T(1,128)S(1)} %reshape.82), channel_id=1, replica_groups=mesh['wide'=8,'narrow'=4] {'wide'}, dimensions={0}, use_global_device_ids=true | all-gather | bytes 294912 | tf_op jit(solution)/shard_map/all_gather | solution.py:11
  192.9 30.9 %all-gather.13 = f32[8,1,8192]{2,1,0:T(1,128)S(1)} all-gather(f32[1,1,8192]{2,1,0:T(1,128)S(1)} %reshape.84), channel_id=1, replica_groups=mesh['wide'=8,'narrow'=4] {'wide'}, dimensions={0}, use_global_device_ids=true | all-gather | bytes 294912 | tf_op jit(solution)/shard_map/all_gather | solution.py:11
  225.5 32.9 %while.170 = (s32[]{:T(128)}, f32[512]{0:T(512)S(1)}, f32[512]{0:T(512)S(1)}, bf16[4,2048,128]{2,1,0:T(8,128)(2,1)}, f32[4,2048]{1,0:T(4,128)S(1)}, /*index=5*/b...) while((s32[]{:T(128)}, f32[512]{0:T(512)S(1)}, ...), condition=%wide.region_29.30_spmd.clone, body=%wide.region_26.29_spmd.clone.sunk | while | flops 554699264 | bytes 31281820 | solution.py:111
  225.5 2.7 fusion.82
  228.2 3.1 exponential_reduce_fusion.14
  231.7 2.0 fusion.84
  233.7 2.7 fusion.82
  236.5 3.1 exponential_reduce_fusion.14
  239.9 2.1 fusion.84
  242.0 2.7 fusion.82
  244.7 3.1 exponential_reduce_fusion.14
  248.2 2.0 fusion.84
  250.2 2.7 fusion.82
  252.9 3.1 exponential_reduce_fusion.14
  256.4 2.1 fusion.84
  258.4 5.2 %all-gather.14 = f32[4,1,512]{2,1,0:T(1,128)S(1)} all-gather(f32[1,1,512]{2,1,0:T(1,128)S(1)} %bitcast.196), channel_id=6, replica_groups=mesh['wide'=8,'narrow'=4] {'narrow'}, dimensions={0}, use_global_device_ids=true | all-gather | bytes 10240 | tf_op jit(solution)/shard_map/all_gather | solution.py:11
  263.6 5.2 %all-gather.15 = f32[4,1,512]{2,1,0:T(1,128)S(1)} all-gather(f32[1,1,512]{2,1,0:T(1,128)S(1)} %bitcast.215), channel_id=7, replica_groups=mesh['wide'=8,'narrow'=4] {'narrow'}, dimensions={0}, use_global_device_ids=true | all-gather | bytes 10240 | tf_op jit(solution)/shard_map/all_gather | solution.py:11
  269.6 7.1 %while.171 = (s32[]{:T(128)}, f32[512,128]{1,0:T(8,128)S(1)}, f32[4,2048]{1,0:T(4,128)S(1)}, bf16[4,2048,128]{2,1,0:T(8,128)(2,1)S(1)}, bf16[512,128]{1,0:T(8,12...) while((s32[]{:T(128)}, f32[512,128]{1,0:T(8,128)S(1)}, f32[4,2048]{1,0:T(4,128)S(1)}, ...), condition=%wide.region_33.34_spmd.clone, body=%wide.region_32.33_spmd.clone.sunk | while | flops 543293440 | bytes 1731683 | solution.py:133
  277.9 32.1 %all-reduce.2.cloned.1.call-done = bf16[512,128]{1,0:T(8,128)(2,1)} async-done(((bf16[512,128]{1,0:T(8,128)(2,1)}), bf16[512,128]{1,0:T(8,128)(2,1)}) %all-reduce.2.cloned.1.call-update) | async-done | bytes 131088 | tf_op jit(solution)/shard_map/psum | solution.py:138
  311.7 39.6 %reduce-scatter.2.cloned.1.call-done = bf16[1024,128]{1,0:T(8,128)(2,1)} async-done(((bf16[8192,128]{1,0:T(8,128)(2,1)}), bf16[1024,128]{1,0:T(8,128)(2,1)}) %reduce-scatter.2.cloned.1.call-update) | async-done | bytes 262160 | tf_op jit(solution)/shard_map/reduce_scatter | solution.py:117
  (213 shorter events, 34.1 us)
Async XLA Ops:
  8.0 7.5 %copy-start.1 = (bf16[512,128]{1,0:T(8,128)(2,1)S(1)}, bf16[512,128]{1,0:T(8,128)(2,1)}, u32[]{:S(2)}) copy-start(bf16[512,128]{1,0:T(8,128)(2,1)} %param.27) | copy-start | bytes 393220
  8.0 7.8 %copy-start.4 = (f32[8192]{0:T(1024)S(1)}, f32[8192]{0:T(1024)}, u32[]{:S(2)}) copy-start(f32[8192]{0:T(1024)} %param.31) | copy-start | bytes 98308
  8.0 302.0 %all-reduce.2.cloned.1.call-start = ((), (), s32[]{:S(2)}) async-start(), calls=%async_computation.1 | async-start | bytes 262144 | tf_op jit(solution)/shard_map/psum | solution.py:138
  15.8 34.5 %copy-start.5 = (f32[512]{0:T(512)S(1)}, f32[512]{0:T(512)}, u32[]{:S(2)}) copy-start(f32[512]{0:T(512)} %param.29) | copy-start | bytes 6148
  50.4 70.8 %copy-start.3 = (f32[8192]{0:T(1024)S(1)}, f32[8192]{0:T(1024)}, u32[]{:S(2)}) copy-start(f32[8192]{0:T(1024)} %param.30) | copy-start | bytes 98308
  224.9 0.6 copy-start.2
  228.2 3.4 copy-start
  236.5 3.4 copy-start
  244.7 3.4 copy-start
  252.9 3.4 copy-start
  277.3 74.1 %reduce-scatter.2.cloned.1.call-start = ((), (), s32[]{:S(2)}) async-start(), calls=%async_computation.2 | async-start | bytes 2359296 | tf_op jit(solution)/shard_map/reduce_scatter | solution.py:117
Sparse Core Ops, SparseCore 0:
  277.4 32.4 all-reduce.1
Sparse Core Ops, SparseCore 1:
  281.3 70.0 reduce-scatter.1
where the time goes:
time: 361 us
  blocking collectives  156 us (43%)
  waiting for transfers between devices  72.3 us (20%)
  matrix products  55.3 us (15%)
  other arithmetic  53.4 us (15%)
  between operations  15.9 us (4%)
  local copies, waits for them, and re-layouts  6.07 us (2%)
    all_gather x10, blocking collectives, combined_all(): gathered = jax.tree.map(lambda a: lax.all_gather(a, axis), part)  156 us
    dot_general x20, matrix products, cost_of(): lax.dot_general(left, right, (((1,), (1,)), ((), ())), preferred_element_...  40.2 us
    reduce_scatter x1, waiting for transfers between devices, on_device(): lax.psum_scatter(tile_sums.reshape(n_cols, feat_width).astype(jnp.bfloat1...  39.6 us
    reduce_sum x12, other arithmetic, row_update(): jnp.sum(jnp.exp(scores - new_high[:, None]), axis=1)  34.8 us
    psum x1, waiting for transfers between devices, on_device(): sums_a = lax.psum(sums_a.astype(jnp.bfloat16), 'narrow').astype(jnp.float32)  32.1 us
    dot_general x4, matrix products, left_product(): lax.dot_general(weights, tile_a, (((0,), (0,)), ((), ())), preferred_elem...  8.21 us
  transfers between devices with their start and end apart: 2, of which 2 were waited for; matrix products, arithmetic and copies ran while one was open for 0% of the time, Pallas kernels for 0%

commit v1 on v0

--- a/solution.py
+++ b/solution.py
@@ -135,7 +135,9 @@
         jnp.zeros((n_rows, feat_width), jnp.float32),
         (b_tiles, potential_b.reshape(n_tiles, col_span)),
     )
-    sums_a = lax.psum(sums_a.astype(jnp.bfloat16), "narrow").astype(jnp.float32)
+    sums_a = jnp.sum(lax.all_gather(sums_a.astype(jnp.bfloat16), "narrow"), axis=0).astype(
+        jnp.float32
+    )
     flow_a = sums_a - unit_a.astype(jnp.float32)
     return (potential_a, potential_b, flow_a, flow_b)
 

time: 361 us -> 337 us (0.934)
  waiting for transfers between devices: 72.3 us -> 43.3 us
  blocking collectives: 156 us -> 164 us
    psum x1 -> x0, waiting for transfers between devices: 32.1 us -> none  [on_device(): sums_a = lax.psum(sums_a.astype(jnp.bfloat16), 'narrow').astype(jnp.float32)]
    all_gather x0 -> x1, blocking collectives: none -> 7.3 us  [on_device(): lax.all_gather(sums_a.astype(jnp.bfloat16), 'narrow')]
  transfers between devices with their start and end apart: 2 -> 1, of which waited for: 2 -> 1; matrix products, arithmetic and copies ran while one was open for 0% -> 3% of each run, Pallas kernels for 0% -> 0%
where the time goes in v1:
time: 337 us; the launch traced here: 336 us
  blocking collectives  164 us (49%)
  matrix products  55.3 us (16%)
  other arithmetic  52 us (15%)
  waiting for transfers between devices  43.3 us (13%)
  between operations  14.4 us (4%)
  local copies, waits for them, and re-layouts  6.07 us (2%)
    all_gather x10, blocking collectives, combined_all(): gathered = jax.tree.map(lambda a: lax.all_gather(a, axis), part)  156 us
    reduce_scatter x1, waiting for transfers between devices, on_device(): lax.psum_scatter(tile_sums.reshape(n_cols, feat_width).astype(jnp.bfloat1...  43.2 us
    dot_general x20, matrix products, cost_of(): lax.dot_general(left, right, (((1,), (1,)), ((), ())), preferred_element_...  40.2 us
    reduce_sum x12, other arithmetic, row_update(): jnp.sum(jnp.exp(scores - new_high[:, None]), axis=1)  34.8 us
    dot_general x4, matrix products, left_product(): lax.dot_general(weights, tile_a, (((0,), (0,)), ((), ())), preferred_elem...  8.25 us
    all_gather x1, blocking collectives, on_device(): lax.all_gather(sums_a.astype(jnp.bfloat16), 'narrow')  7.3 us
    dot_general x4, matrix products, flow_tile(): jnp.dot(weights, tile_b, preferred_element_type=jnp.float32)  6.86 us
  transfers between devices with their start and end apart: 1, of which 1 were waited for; matrix products, arithmetic and copies ran while one was open for 3% of the time, Pallas kernels for 0%

profile of v1, /device:TPU:0, one launch (start us, length us, event | category | flops | bytes accessed | tf_op | source)
XLA Modules:
  0.0 335.9 jit_solution(12819288322962061409)
XLA Ops:
  7.2 2.7 fusion.36
  10.0 4.6 %fusion.37 = bf16[8192,128]{1,0:T(8,128)(2,1)S(1)} fusion(bf16[8192,128]{1,0:T(8,128)(2,1)} %param.28, f32[8192]{0:T(1024)S(1)} %add_sqrt_fusion), kind=kLoop, calls=%fused_computation.76 | loop fusion | flops 3145728 | bytes 4227072 | tf_op jit(solution)/shard_map/convert_element_type | solution.py:23
  15.0 22.7 %while.168 = (s32[]{:T(128)}, f32[512]{0:T(512)S(1)}, f32[512]{0:T(512)S(1)}, f32[4,2048]{1,0:T(4,128)S(1)}, bf16[4,2048,128]{2,1,0:T(8,128)(2,1)S(1)}, /*index=5*/bf16[512,128]{1,0:T(8,128)(2,1)S(1)}, s32[]{:T(128)}, s32[]{:T(128)}) while((s32[]{:T(128)}, f32[512]{0:T(512)S(1)}, f32[512]{0:T(512)S(1)}, f32[4,2048]{1,0:T(4,128)S(1)}, ...), condition=%wide.region_5.6_spmd.clone, body=%wide.region_2.5_spmd.clone.sunk | while | flops 275778048 | bytes 9095272 | solution.py:84
  15.0 2.8 fusion.75
  17.8 2.8 exponential_reduce_fusion.12
  20.7 2.8 fusion.75
  23.5 2.8 exponential_reduce_fusion.12
  26.4 2.8 fusion.75
  29.2 2.8 exponential_reduce_fusion.12
  32.0 2.8 fusion.75
  34.8 2.8 exponential_reduce_fusion.12
  37.7 6.2 %all-gather.7 = f32[4,1,512]{2,1,0:T(1,128)S(1)} all-gather(f32[1,1,512]{2,1,0:T(1,128)S(1)} %bitcast.200), channel_id=2, replica_groups=mesh['wide'=8,'narrow'=4] {'narrow'}, dimensions={0}, use_global_device_ids=true | all-gather | bytes 10240 | tf_op jit(solution)/shard_map/all_gather | solution.py:11
  43.9 5.5 %all-gather.8 = f32[4,1,512]{2,1,0:T(1,128)S(1)} all-gather(f32[1,1,512]{2,1,0:T(1,128)S(1)} %bitcast.219), channel_id=3, replica_groups=mesh['wide'=8,'narrow'=4] {'narrow'}, dimensions={0}, use_global_device_ids=true | all-gather | bytes 10240 | tf_op jit(solution)/shard_map/all_gather | solution.py:11
  49.6 7.3 %while.162 = (s32[]{:T(128)}, f32[4,2048]{1,0:T(4,128)S(1)}, f32[4,2048]{1,0:T(4,128)S(1)}, f32[512]{0:T(512)S(1)}, bf16[4,2048,128]{2,1,0:T(8,128)(2,1)S(1)}, /...) while((s32[]{:T(128)}, f32[4,2048]{1,0:T(4,128)S(1)}, f32[4,2048]{1,0:T(4,128)S(1)}, ...), condition=%wide.region_11.12_spmd, body=%wide.region_8.11_spmd.sunk | while | flops 275771392 | bytes 9103457 | solution.py:98
  56.9 31.4 %all-gather.9 = f32[8,1,8192]{2,1,0:T(1,128)S(1)} all-gather(f32[1,1,8192]{2,1,0:T(1,128)S(1)} %reshape.75), channel_id=1, replica_groups=mesh['wide'=8,'narrow'=4] {'wide'}, dimensions={0}, use_global_device_ids=true | all-gather | bytes 294912 | tf_op jit(solution)/shard_map/all_gather | solution.py:11
  88.6 30.7 %all-gather.10 = f32[8,1,8192]{2,1,0:T(1,128)S(1)} all-gather(f32[1,1,8192]{2,1,0:T(1,128)S(1)} %reshape.77), channel_id=1, replica_groups=mesh['wide'=8,'narrow'=4] {'wide'}, dimensions={0}, use_global_device_ids=true | all-gather | bytes 294912 | tf_op jit(solution)/shard_map/all_gather | solution.py:11
  120.4 22.7 %while.169 = (s32[]{:T(128)}, f32[512]{0:T(512)S(1)}, f32[512]{0:T(512)S(1)}, f32[4,2048]{1,0:T(4,128)S(1)}, bf16[4,2048,128]{2,1,0:T(8,128)(2,1)S(1)}, /*index=5*/bf16[512,128]{1,0:T(8,128)(2,1)S(1)}, s32[]{:T(128)}, s32[]{:T(128)}) while((s32[]{:T(128)}, f32[512]{0:T(512)S(1)}, f32[512]{0:T(512)S(1)}, ...), condition=%wide.region_17.18_spmd.clone, body=%wide.region_14.17_spmd.clone.sunk | while | flops 275778048 | bytes 9095272 | solution.py:84
  120.4 2.8 fusion.78
  123.2 2.8 exponential_reduce_fusion.13
  126.1 2.8 fusion.78
  128.9 2.8 exponential_reduce_fusion.13
  131.7 2.8 fusion.78
  134.5 2.8 exponential_reduce_fusion.13
  137.4 2.8 fusion.78
  140.2 2.8 exponential_reduce_fusion.13
  143.1 5.2 %all-gather.11 = f32[4,1,512]{2,1,0:T(1,128)S(1)} all-gather(f32[1,1,512]{2,1,0:T(1,128)S(1)} %bitcast.199), channel_id=4, replica_groups=mesh['wide'=8,'narrow'=4] {'narrow'}, dimensions={0}, use_global_device_ids=true | all-gather | bytes 10240 | tf_op jit(solution)/shard_map/all_gather | solution.py:11
  148.3 5.2 %all-gather.12 = f32[4,1,512]{2,1,0:T(1,128)S(1)} all-gather(f32[1,1,512]{2,1,0:T(1,128)S(1)} %bitcast.218), channel_id=5, replica_groups=mesh['wide'=8,'narrow'=4] {'narrow'}, dimensions={0}, use_global_device_ids=true | all-gather | bytes 10240 | tf_op jit(solution)/shard_map/all_gather | solution.py:11
  153.6 7.3 %while.165 = (s32[]{:T(128)}, f32[4,2048]{1,0:T(4,128)S(1)}, f32[4,2048]{1,0:T(4,128)S(1)}, f32[512]{0:T(512)S(1)}, bf16[4,2048,128]{2,1,0:T(8,128)(2,1)S(1)}, /...) while((s32[]{:T(128)}, f32[4,2048]{1,0:T(4,128)S(1)}, f32[4,2048]{1,0:T(4,128)S(1)}, ...), condition=%wide.region_23.24_spmd, body=%wide.region_20.23_spmd.sunk | while | flops 275771392 | bytes 9103457 | solution.py:98
  161.0 30.8 %all-gather.13 = f32[8,1,8192]{2,1,0:T(1,128)S(1)} all-gather(f32[1,1,8192]{2,1,0:T(1,128)S(1)} %reshape.83), channel_id=1, replica_groups=mesh['wide'=8,'narrow'=4] {'wide'}, dimensions={0}, use_global_device_ids=true | all-gather | bytes 294912 | tf_op jit(solution)/shard_map/all_gather | solution.py:11
  192.0 30.9 %all-gather.14 = f32[8,1,8192]{2,1,0:T(1,128)S(1)} all-gather(f32[1,1,8192]{2,1,0:T(1,128)S(1)} %reshape.85), channel_id=1, replica_groups=mesh['wide'=8,'narrow'=4] {'wide'}, dimensions={0}, use_global_device_ids=true | all-gather | bytes 294912 | tf_op jit(solution)/shard_map/all_gather | solution.py:11
  224.6 33.0 %while.170 = (s32[]{:T(128)}, f32[512]{0:T(512)S(1)}, f32[512]{0:T(512)S(1)}, bf16[4,2048,128]{2,1,0:T(8,128)(2,1)}, f32[4,2048]{1,0:T(4,128)S(1)}, /*index=5*/b...) while((s32[]{:T(128)}, f32[512]{0:T(512)S(1)}, ...), condition=%wide.region_29.30_spmd.clone, body=%wide.region_26.29_spmd.clone.sunk | while | flops 554699264 | bytes 31281820 | solution.py:111
  224.6 2.7 fusion.82
  227.4 3.1 exponential_reduce_fusion.14
  230.8 2.0 fusion.84
  232.9 2.7 fusion.82
  235.6 3.1 exponential_reduce_fusion.14
  239.0 2.1 fusion.84
  241.1 2.7 fusion.82
  243.8 3.1 exponential_reduce_fusion.14
  247.3 2.1 fusion.84
  249.4 2.7 fusion.82
  252.1 3.1 exponential_reduce_fusion.14
  255.5 2.1 fusion.84
  257.6 5.2 %all-gather.15 = f32[4,1,512]{2,1,0:T(1,128)S(1)} all-gather(f32[1,1,512]{2,1,0:T(1,128)S(1)} %bitcast.198), channel_id=6, replica_groups=mesh['wide'=8,'narrow'=4] {'narrow'}, dimensions={0}, use_global_device_ids=true | all-gather | bytes 10240 | tf_op jit(solution)/shard_map/all_gather | solution.py:11
  262.8 5.2 %all-gather.16 = f32[4,1,512]{2,1,0:T(1,128)S(1)} all-gather(f32[1,1,512]{2,1,0:T(1,128)S(1)} %bitcast.217), channel_id=7, replica_groups=mesh['wide'=8,'narrow'=4] {'narrow'}, dimensions={0}, use_global_device_ids=true | all-gather | bytes 10240 | tf_op jit(solution)/shard_map/all_gather | solution.py:11
  268.7 7.0 %while.171 = (s32[]{:T(128)}, f32[512,128]{1,0:T(8,128)S(1)}, f32[4,2048]{1,0:T(4,128)S(1)}, bf16[4,2048,128]{2,1,0:T(8,128)(2,1)S(1)}, bf16[512,128]{1,0:T(8,12...) while((s32[]{:T(128)}, f32[512,128]{1,0:T(8,128)S(1)}, f32[4,2048]{1,0:T(4,128)S(1)}, ...), condition=%wide.region_33.34_spmd.clone, body=%wide.region_32.33_spmd.clone.sunk | while | flops 543293440 | bytes 1731683 | solution.py:133
  275.8 7.3 %all-gather.6 = bf16[2048,128]{1,0:T(8,128)(2,1)S(1)} all-gather(bf16[512,128]{1,0:T(8,128)(2,1)S(1)} %convert_element_type.45), channel_id=8, replica_groups=mesh['wide'=8,'narrow'=4] {'narrow'}, dimensions={0}, use_global_device_ids=true | all-gather | bytes 655360 | tf_op jit(solution)/shard_map/all_gather | solution.py:138
  284.0 43.2 %reduce-scatter.2.cloned.1.call-done = bf16[1024,128]{1,0:T(8,128)(2,1)} async-done(((bf16[8192,128]{1,0:T(8,128)(2,1)}), bf16[1024,128]{1,0:T(8,128)(2,1)}) %reduce-scatter.2.cloned.1.call-update) | async-done | bytes 262160 | tf_op jit(solution)/shard_map/reduce_scatter | solution.py:117
  (212 shorter events, 31.9 us)
Async XLA Ops:
  7.2 7.5 %copy-start.1 = (bf16[512,128]{1,0:T(8,128)(2,1)S(1)}, bf16[512,128]{1,0:T(8,128)(2,1)}, u32[]{:S(2)}) copy-start(bf16[512,128]{1,0:T(8,128)(2,1)} %param.27) | copy-start | bytes 393220
  7.2 7.8 %copy-start.4 = (f32[8192]{0:T(1024)S(1)}, f32[8192]{0:T(1024)}, u32[]{:S(2)}) copy-start(f32[8192]{0:T(1024)} %param.31) | copy-start | bytes 98308
  7.2 320.1 %reduce-scatter.2.cloned.1.call-start = ((), (), s32[]{:S(2)}) async-start(), calls=%async_computation.1 | async-start | bytes 2359296 | tf_op jit(solution)/shard_map/reduce_scatter | solution.py:117
  15.0 34.5 %copy-start.5 = (f32[512]{0:T(512)S(1)}, f32[512]{0:T(512)}, u32[]{:S(2)}) copy-start(f32[512]{0:T(512)} %param.29) | copy-start | bytes 6148
  49.6 70.8 %copy-start.3 = (f32[8192]{0:T(1024)S(1)}, f32[8192]{0:T(1024)}, u32[]{:S(2)}) copy-start(f32[8192]{0:T(1024)} %param.30) | copy-start | bytes 98308
  224.0 0.6 copy-start.2
  227.3 3.4 %copy-start = (f32[2048,512]{1,0:T(8,128)S(1)}, f32[2048,512]{1,0:T(8,128)}, u32[]{:S(2)}) copy-start(f32[2048,512]{1,0:T(8,128)} %get-tuple-element.1612) | copy-start | bytes 12582916 | tf_op jit(solution)/shard_map/while
  235.6 3.4 %copy-start = (f32[2048,512]{1,0:T(8,128)S(1)}, f32[2048,512]{1,0:T(8,128)}, u32[]{:S(2)}) copy-start(f32[2048,512]{1,0:T(8,128)} %get-tuple-element.1612) | copy-start | bytes 12582916 | tf_op jit(solution)/shard_map/while
  243.8 3.4 %copy-start = (f32[2048,512]{1,0:T(8,128)S(1)}, f32[2048,512]{1,0:T(8,128)}, u32[]{:S(2)}) copy-start(f32[2048,512]{1,0:T(8,128)} %get-tuple-element.1612) | copy-start | bytes 12582916 | tf_op jit(solution)/shard_map/while
  252.1 3.4 %copy-start = (f32[2048,512]{1,0:T(8,128)S(1)}, f32[2048,512]{1,0:T(8,128)}, u32[]{:S(2)}) copy-start(f32[2048,512]{1,0:T(8,128)} %get-tuple-element.1612) | copy-start | bytes 12582916 | tf_op jit(solution)/shard_map/while
Sparse Core Ops, SparseCore 0:
  257.7 69.4 reduce-scatter.1
